TPU v7x, 128 devices: a whole 4x4x4 slice. The times are simulated.
128 devices in a mesh: pair: 16 (over x, z_lo, core), aux: 8 (over y, z_hi).
Axes of the slice: x: 4, y: 4, z: 4 (z_hi: 2, z_lo: 2; z = z_hi * 2 + z_lo), core: 2. Of those that a mesh axis runs over, the one named last changes fastest.
Arguments:
- integrals: bfloat16 [16, 2, 512, 256, 256], P('pair', None, 'aux'), may hold values from -6 to 6
- coef_table: bfloat16 [2048, 2, 128], P('pair'), may hold values from -0.375 to 0.375
- row_slot: int32 [2048], replicated, may hold values from 0 to 2047, each once
- pair_k: int32 [16, 2], P('pair'), may hold values from 0 to 7, as said below
Outputs:
- exchange_k: float32 [2, 8, 256, 256], P(None, None, 'aux', 'pair')
Inputs may be any that keep to these rules, and one draw needn't show every extreme that they name: `row_slot`: each table row holds exactly one orbital row of one k-point. `pair_k`: the two k-points of a pair differ, and every k-point belongs to some listed pair.
All inputs are finite; a program needn't handle non-finite values.
Results may differ from a plain program's by a relative error of at most 0.0003.
Values may be sent and summed in bfloat16 or wider, within the bound.
A program may use at most 192 MiB of HBM per device.

v0:
```python
import jax
import jax.numpy as jnp
from jax import lax
from jax.sharding import PartitionSpec as P

NKPT = 8


def pick_rows(gathered, row_slot, kpoint, norbitals):
    slots = lax.dynamic_slice_in_dim(row_slot, kpoint * norbitals, norbitals)
    return gathered[slots].reshape(norbitals, -1)


def exchange_block(real_part, imag_part, factor):
    rounded_real = real_part.astype(jnp.bfloat16)
    rounded_imag = imag_part.astype(jnp.bfloat16)
    joined = jnp.concatenate([rounded_real, rounded_imag], -1)
    turned = jnp.concatenate([rounded_imag, -rounded_real], -1)
    k_real = jnp.einsum("pmj,plj->ml", joined, joined, preferred_element_type=jnp.float32)
    k_imag = jnp.einsum("pmj,plj->ml", turned, joined, preferred_element_type=jnp.float32)
    return jnp.stack([k_real, k_imag]) * factor


def local(integrals, coef_table, row_slot, pair_k):
    gathered = lax.all_gather(coef_table, "pair", axis=0, tiled=True)
    norbitals = integrals.shape[-1]
    noccupied = coef_table.shape[-1]
    factor = 1.0 / (integrals.shape[2] * lax.axis_size("aux") * noccupied)
    blocks = integrals[0]
    first_k = pair_k[0, 0]
    second_k = pair_k[0, 1]
    coeff_second = pick_rows(gathered, row_slot, second_k, norbitals)
    coeff_first = pick_rows(gathered, row_slot, first_k, norbitals)
    flat_blocks = blocks.reshape(-1, norbitals)
    product = jnp.dot(flat_blocks, coeff_second, preferred_element_type=jnp.float32)
    product = product.reshape(blocks.shape[:-1] + (2 * noccupied,))
    left_real = product[0, ..., :noccupied] - product[1, ..., noccupied:]
    left_imag = product[0, ..., noccupied:] + product[1, ..., :noccupied]
    first_block = exchange_block(left_real, left_imag, factor)
    product = jnp.einsum("cpmn,mj->cpnj", blocks, coeff_first, preferred_element_type=jnp.float32)
    right_real = product[0, ..., :noccupied] + product[1, ..., noccupied:]
    right_imag = product[0, ..., noccupied:] - product[1, ..., :noccupied]
    second_block = exchange_block(right_real, right_imag, factor)
    kpoints = jnp.arange(NKPT, dtype=jnp.int32)
    first_hot = (kpoints == first_k).astype(jnp.float32)[None, :, None, None]
    second_hot = (kpoints == second_k).astype(jnp.float32)[None, :, None, None]
    spread = first_block[:, None] * first_hot + second_block[:, None] * second_hot
    summed = lax.psum_scatter(spread, "pair", scatter_dimension=3, tiled=True)
    return lax.psum_scatter(summed, "aux", scatter_dimension=2, tiled=True)


def solution(mesh):
    in_specs = (P("pair", None, "aux", None, None), P("pair", None, None), P(), P("pair", None))
    out_specs = P(None, None, "aux", "pair")
    return jax.shard_map(local, mesh=mesh, in_specs=in_specs, out_specs=out_specs, check_vma=False)
```

profile of v0, /device:TPU:0, one launch (start us, length us, event | category | flops | bytes accessed | tf_op | source)
XLA Modules:
  0.0 333.2 jit_solution(5182410068761711925)
XLA Ops:
  7.3 1.4 fusion.37
  10.0 1.3 compare_convert_fusion
  12.0 31.7 %all-gather.2.cloned.1.call-done = bf16[2048,2,128]{2,1,0:T(2,128)(2,1)} async-done(((bf16[128,2,128]{2,1,0:T(2,128)(2,1)}), bf16[2048,2,128]{2,1,0:T(2,128)(2,1)}) %all-gather.2.cloned.1.call-update) | async-done | bytes 1048592 | tf_op jit(solution)/shard_map/all_gather | solution.py:25
  43.7 2.2 gather_fusion.1
  46.0 18.9 %convolution_bitcast_fusion.1 = f32[2,64,256,256]{2,3,1,0:T(8,128)} fusion(bf16[256,256,1,1]{0,1,3,2:T(8,128)(2,1)S(1)} %bitcast.55, bf16[1,2,64,256,256]{4,3,2,1,0:T(8,128)(2,1)} %param.4), kind=kOutput, calls=%fused_computation.3 | convolution fusion | flops 4294967296 | bytes 50462720 | tf_op jit(solution)/shard_map/cpmn,mj->cpnj/dot_general | solution.py:40
  64.9 8.8 %fusion.18 = bf16[64,256,128]{1,2,0:T(8,128)(2,1)} fusion(f32[2,64,256,256]{2,3,1,0:T(8,128)} %convolution_bitcast_fusion.1), kind=kLoop, calls=%fused_computation.28 | loop fusion | flops 4194304 | bytes 20971520 | tf_op jit(solution)/shard_map/convert_element_type | solution.py:16
  73.7 9.8 %fusion.35 = (bf16[64,256,128]{1,2,0:T(8,128)(2,1)}, bf16[64,256,128]{1,2,0:T(8,128)(2,1)}) fusion(f32[2,64,256,256]{2,3,1,0:T(8,128)} %convolution_bitcast_fusion.1), kind=kLoop, calls=%fused_computation.49 | loop fusion | flops 6291456 | bytes 25165824 | tf_op jit(solution)/shard_map/neg | solution.py:18
  83.6 2.2 gather_fusion
  85.7 24.4 %convolution_bitcast_fusion = f32[32768,256]{0,1:T(8,128)} fusion(bf16[32768,256]{1,0:T(8,128)(2,1)} %bitcast.51, bf16[32,8,2,128]{3,2,1,0:T(2,128)(2,1)S(1)} %bitcast.53), kind=kOutput, calls=%fused_computation.2 | convolution fusion | flops 4294967296 | bytes 50462720 | tf_op jit(solution)/shard_map/dot_general | solution.py:35
  110.1 33.4 %copy.35 = f32[32768,256]{1,0:T(8,128)} copy(f32[32768,256]{0,1:T(8,128)} %convolution_bitcast_fusion) | data formatting | bytes 67108864 | tf_op jit(solution)/shard_map/reshape | solution.py:36
  143.6 8.6 %fusion.16 = bf16[64,256,128]{2,1,0:T(8,128)(2,1)} fusion(f32[2,64,256,256]{3,2,1,0:T(8,128)} %bitcast.49), kind=kLoop, calls=%fused_computation.26 | loop fusion | flops 4194304 | bytes 20971520 | tf_op jit(solution)/shard_map/convert_element_type | solution.py:16
  152.2 10.0 %fusion.33 = (bf16[64,256,128]{2,1,0:T(8,128)(2,1)}, bf16[64,256,128]{2,1,0:T(8,128)(2,1)}) fusion(f32[2,64,256,256]{3,2,1,0:T(8,128)} %bitcast.50), kind=kLoop, calls=%fused_computation.48 | loop fusion | flops 6291456 | bytes 25165824 | tf_op jit(solution)/shard_map/neg | solution.py:18
  162.2 1.4 copy-done.3
  163.5 2.4 fusion.20
  165.9 2.4 fusion.21
  168.6 8.4 %fusion.19 = f32[1,256,256]{2,1,0:T(8,128)S(1)} fusion(bf16[64,256,128]{2,1,0:T(8,128)(2,1)} %fusion.16, bf16[64,256,128]{2,1,0:T(8,128)(2,1)} %get-tuple-element.6), kind=kOutput, calls=%fused_computation.30 | convolution fusion | flops 2164260864 | bytes 8650752 | tf_op jit(solution)/shard_map/pmj,plj->ml/dot_general | solution.py:19
  177.0 1.1 copy-done.5
  178.0 2.4 fusion.24
  180.6 2.6 multiply_add_fusion
  183.3 68.2 %reduce-scatter.5.cloned.1.call-done = f32[2,8,256,16]{2,3,1,0:T(8,128)} async-done(((f32[2,8,256,256]{2,3,1,0:T(8,128)}), f32[2,8,256,16]{2,3,1,0:T(8,128)}) %reduce-scatter.5.cloned.1.call-update) | async-done | bytes 262160 | tf_op jit(solution)/shard_map/reduce_scatter | solution.py:48
  251.5 2.2 copy.33
  253.8 1.5 reshape.87
  255.3 69.6 %reduce-scatter.7.cloned.1.call-done = f32[32,256]{1,0:T(8,128)} async-done(((f32[256,256]{1,0:T(8,128)}), f32[32,256]{1,0:T(8,128)}) %reduce-scatter.7.cloned.1.call-update) | async-done | bytes 32784
  325.0 0.9 reshape.88
  (24 shorter events, 3.0 us)
Async XLA Ops:
  6.5 37.2 %all-gather.2.cloned.1.call-start = ((), (), s32[]{:S(2)}) async-start(), calls=%async_computation.2 | async-start | bytes 1114112 | tf_op jit(solution)/shard_map/all_gather | solution.py:25
  7.3 244.3 %reduce-scatter.5.cloned.1.call-start = ((), (), s32[]{:S(2)}) async-start(), calls=%async_computation.3 | async-start | bytes 4456448 | tf_op jit(solution)/shard_map/reduce_scatter | solution.py:48
  152.2 10.0 %copy-start = (bf16[64,256,128]{1,2,0:T(8,128)(2,1)S(1)}, bf16[64,256,128]{1,2,0:T(8,128)(2,1)}, u32[]{:S(2)}) copy-start(bf16[64,256,128]{1,2,0:T(8,128)(2,1)} %fusion.18) | copy-start | bytes 12582916
  152.2 11.3 %copy-start.3 = (bf16[64,256,128]{1,2,0:T(8,128)(2,1)S(1)}, bf16[64,256,128]{1,2,0:T(8,128)(2,1)}, u32[]{:S(2)}) copy-start(bf16[64,256,128]{1,2,0:T(8,128)(2,1)} %get-tuple-element.8) | copy-start | bytes 12582916
  163.5 2.4 copy-start.2
  168.5 8.4 %copy-start.1 = (bf16[64,256,128]{2,1,0:T(8,128)(2,1)S(1)}, bf16[64,256,128]{2,1,0:T(8,128)(2,1)}, u32[]{:S(2)}) copy-start(bf16[64,256,128]{2,1,0:T(8,128)(2,1)} %fusion.16) | copy-start | bytes 12582916
  168.5 8.4 %copy-start.4 = (bf16[64,256,128]{2,1,0:T(8,128)(2,1)S(1)}, bf16[64,256,128]{2,1,0:T(8,128)(2,1)}, u32[]{:S(2)}) copy-start(bf16[64,256,128]{2,1,0:T(8,128)(2,1)} %get-tuple-element.5) | copy-start | bytes 12582916
  168.5 9.5 %copy-start.5 = (bf16[64,256,128]{2,1,0:T(8,128)(2,1)S(1)}, bf16[64,256,128]{2,1,0:T(8,128)(2,1)}, u32[]{:S(2)}) copy-start(bf16[64,256,128]{2,1,0:T(8,128)(2,1)} %get-tuple-element.6) | copy-start | bytes 12582916
  183.2 141.7 %reduce-scatter.7.cloned.1.call-start = ((), (), s32[]{:S(2)}) async-start(), calls=%async_computation.4 | async-start | bytes 294912
Sparse Core Ops, SparseCore 0:
  9.0 34.6 all-gather.1
  183.4 68.1 reduce-scatter.4
  255.4 69.4 reduce-scatter.6
where the time goes:
time: 334 us; the launch traced here: 333 us
  waiting for transfers between devices  170 us (51%)
  matrix products  58.8 us (18%)
  local copies, waits for them, and re-layouts  47.5 us (14%)
  other arithmetic  41.9 us (13%)
  between operations  14.6 us (4%)
    unnamed x4, waiting for transfers between devices  70.4 us
    reduce_scatter x1, waiting for transfers between devices, local(): summed = lax.psum_scatter(spread, 'pair', scatter_dimension=3, tiled=True)  68.2 us
    reshape x1, local copies, waits for them, and re-layouts, local(): product = product.reshape(blocks.shape[:-1] + (2 * noccupied,))  33.4 us
    all_gather x1, waiting for transfers between devices, local(): gathered = lax.all_gather(coef_table, 'pair', axis=0, tiled=True)  31.7 us
    dot_general x1, matrix products, local(): jnp.dot(flat_blocks, coeff_second, preferred_element_type=jnp.float32)  24.4 us
    neg x2, other arithmetic, exchange_block(): turned = jnp.concatenate([rounded_imag, -rounded_real], -1)  19.8 us
    dot_general x1, matrix products, local(): jnp.einsum('cpmn,mj->cpnj', blocks, coeff_first, preferred_element_type=j...  18.9 us
    convert_element_type x2, other arithmetic, exchange_block(): rounded_imag = imag_part.astype(jnp.bfloat16)  17.4 us
  transfers between devices with their start and end apart: 3, of which 3 were waited for; matrix products, arithmetic and copies ran while one was open for 1% of the time, Pallas kernels for 0%

commit v1 on v0

--- a/solution.py
+++ b/solution.py
@@ -22,7 +22,10 @@
 
 
 def local(integrals, coef_table, row_slot, pair_k):
-    gathered = lax.all_gather(coef_table, "pair", axis=0, tiled=True)
+    set_lane = lambda xx: jnp.concatenate(
+        lax.all_to_all(jnp.stack([xx] * lax.psum(1, "pair")), "pair", 0, 0), axis=0
+    )
+    gathered = set_lane(coef_table)
     norbitals = integrals.shape[-1]
     noccupied = coef_table.shape[-1]
     factor = 1.0 / (integrals.shape[2] * lax.axis_size("aux") * noccupied)

time: 334 us -> 320 us (0.958)
  waiting for transfers between devices: 170 us -> 150 us
  starting transfers between devices: 0.08 us -> 5.95 us
    all_gather x1 -> x0, waiting for transfers between devices: 31.7 us -> none  [local(): gathered = lax.all_gather(coef_table, 'pair', axis=0, tiled=True)]
    all_to_all x0 -> x1, waiting for transfers between devices: none -> 11.5 us  [local(): lax.all_to_all(jnp.stack([xx] * lax.psum(1, 'pair')), 'pair', 0, 0)]
    all_to_all x0 -> x1, starting transfers between devices: none -> 5.87 us  [local(): lax.all_to_all(jnp.stack([xx] * lax.psum(1, 'pair')), 'pair', 0, 0)]
    unnamed x4 -> x3, waiting for transfers between devices: 70.4 us -> 69.8 us
where the time goes in v1:
time: 320 us; the launch traced here: 319 us
  waiting for transfers between devices  150 us (47%)
  matrix products  58.8 us (18%)
  local copies, waits for them, and re-layouts  47.7 us (15%)
  other arithmetic  42 us (13%)
  between operations  14.9 us (5%)
  starting transfers between devices  5.95 us (2%)
    unnamed x3, waiting for transfers between devices  69.8 us
    reduce_scatter x1, waiting for transfers between devices, local(): summed = lax.psum_scatter(spread, 'pair', scatter_dimension=3, tiled=True)  68.3 us
    reshape x1, local copies, waits for them, and re-layouts, local(): product = product.reshape(blocks.shape[:-1] + (2 * noccupied,))  33.4 us
    dot_general x1, matrix products, local(): jnp.dot(flat_blocks, coeff_second, preferred_element_type=jnp.float32)  24.4 us
    neg x2, other arithmetic, exchange_block(): turned = jnp.concatenate([rounded_imag, -rounded_real], -1)  19.8 us
    dot_general x1, matrix products, local(): jnp.einsum('cpmn,mj->cpnj', blocks, coeff_first, preferred_element_type=j...  19 us
    convert_element_type x2, other arithmetic, exchange_block(): rounded_imag = imag_part.astype(jnp.bfloat16)  17.4 us
    all_to_all x1, waiting for transfers between devices, local(): lax.all_to_all(jnp.stack([xx] * lax.psum(1, 'pair')), 'pair', 0, 0)  11.5 us
  transfers between devices with their start and end apart: 3, of which 3 were waited for; matrix products, arithmetic and copies ran while one was open for 1% of the time, Pallas kernels for 0%

profile of v1, /device:TPU:0, one launch (start us, length us, event | category | flops | bytes accessed | tf_op | source)
XLA Modules:
  0.0 319.0 jit_solution(10913848812313580773)
XLA Ops:
  6.5 2.6 stack.14
  9.2 5.9 %all-to-all-start = ((bf16[16,128,2,128]{3,2,1,0:T(2,128)(2,1)}), bf16[16,128,2,128]{3,2,1,0:T(2,128)(2,1)S(1)}, u32[]{:S(2)}, u32[]{:S(2)}) async-start(bf16[16,128,2,128]{3,2,1,0:T(2,128)(2,1)} %stack.14), calls=%async_computation | async-start | bytes 2097152 | tf_op jit(solution)/shard_map/all_to_all | solution.py:26
  15.1 1.4 fusion.37
  17.8 1.3 compare_convert_fusion
  20.0 11.5 %all-to-all-done = bf16[16,128,2,128]{3,2,1,0:T(2,128)(2,1)S(1)} async-done(((bf16[16,128,2,128]{3,2,1,0:T(2,128)(2,1)}), bf16[16,128,2,128]{3,2,1,0:T(2,128)(2,1)S(1)}, u32[]{:S(2)}, u32[]{:S(2)}) %all-to-all-start) | async-done | bytes 1048608 | tf_op jit(solution)/shard_map/all_to_all | solution.py:26
  31.5 0.9 gather_fusion.1
  32.5 19.0 %convolution_bitcast_fusion.1 = f32[2,64,256,256]{2,3,1,0:T(8,128)} fusion(bf16[256,256,1,1]{0,1,3,2:T(8,128)(2,1)S(1)} %bitcast.58, bf16[1,2,64,256,256]{4,3,2,1,0:T(8,128)(2,1)} %param.4), kind=kOutput, calls=%fused_computation.3 | convolution fusion | flops 4294967296 | bytes 50462720 | tf_op jit(solution)/shard_map/cpmn,mj->cpnj/dot_general | solution.py:43
  51.5 8.8 %fusion.18 = bf16[64,256,128]{1,2,0:T(8,128)(2,1)} fusion(f32[2,64,256,256]{2,3,1,0:T(8,128)} %convolution_bitcast_fusion.1), kind=kLoop, calls=%fused_computation.28 | loop fusion | flops 4194304 | bytes 20971520 | tf_op jit(solution)/shard_map/convert_element_type | solution.py:16
  60.3 9.8 %fusion.35 = (bf16[64,256,128]{1,2,0:T(8,128)(2,1)}, bf16[64,256,128]{1,2,0:T(8,128)(2,1)}) fusion(f32[2,64,256,256]{2,3,1,0:T(8,128)} %convolution_bitcast_fusion.1), kind=kLoop, calls=%fused_computation.49 | loop fusion | flops 6291456 | bytes 25165824 | tf_op jit(solution)/shard_map/neg | solution.py:18
  71.1 24.4 %convolution_bitcast_fusion = f32[32768,256]{0,1:T(8,128)} fusion(bf16[32768,256]{1,0:T(8,128)(2,1)} %bitcast.52, bf16[32,8,2,128]{3,2,1,0:T(2,128)(2,1)S(1)} %bitcast.56), kind=kOutput, calls=%fused_computation.2 | convolution fusion | flops 4294967296 | bytes 50462720 | tf_op jit(solution)/shard_map/dot_general | solution.py:38
  95.4 33.4 %copy.45 = f32[32768,256]{1,0:T(8,128)} copy(f32[32768,256]{0,1:T(8,128)} %convolution_bitcast_fusion) | data formatting | bytes 67108864 | tf_op jit(solution)/shard_map/reshape | solution.py:39
  128.9 8.6 %fusion.16 = bf16[64,256,128]{2,1,0:T(8,128)(2,1)} fusion(f32[2,64,256,256]{3,2,1,0:T(8,128)} %bitcast.50), kind=kLoop, calls=%fused_computation.26 | loop fusion | flops 4194304 | bytes 20971520 | tf_op jit(solution)/shard_map/convert_element_type | solution.py:16
  137.5 10.0 %fusion.33 = (bf16[64,256,128]{2,1,0:T(8,128)(2,1)}, bf16[64,256,128]{2,1,0:T(8,128)(2,1)}) fusion(f32[2,64,256,256]{3,2,1,0:T(8,128)} %bitcast.51), kind=kLoop, calls=%fused_computation.48 | loop fusion | flops 6291456 | bytes 25165824 | tf_op jit(solution)/shard_map/neg | solution.py:18
  147.5 1.4 copy-done.3
  148.8 2.4 fusion.20
  151.2 2.4 fusion.21
  153.9 8.4 %fusion.19 = f32[1,256,256]{2,1,0:T(8,128)S(1)} fusion(bf16[64,256,128]{2,1,0:T(8,128)(2,1)} %fusion.16, bf16[64,256,128]{2,1,0:T(8,128)(2,1)} %get-tuple-element.6), kind=kOutput, calls=%fused_computation.30 | convolution fusion | flops 2164260864 | bytes 8650752 | tf_op jit(solution)/shard_map/pmj,plj->ml/dot_general | solution.py:19
  162.2 1.1 copy-done.5
  163.3 2.4 fusion.24
  166.0 2.6 multiply_add_fusion
  168.6 68.3 %reduce-scatter.5.cloned.1.call-done = f32[2,8,256,16]{2,3,1,0:T(8,128)} async-done(((f32[2,8,256,256]{2,3,1,0:T(8,128)}), f32[2,8,256,16]{2,3,1,0:T(8,128)}) %reduce-scatter.5.cloned.1.call-update) | async-done | bytes 262160 | tf_op jit(solution)/shard_map/reduce_scatter | solution.py:51
  236.9 2.2 copy.43
  239.1 1.5 reshape.93
  240.7 69.8 %reduce-scatter.7.cloned.1.call-done = f32[32,256]{1,0:T(8,128)} async-done(((f32[256,256]{1,0:T(8,128)}), f32[32,256]{1,0:T(8,128)}) %reduce-scatter.7.cloned.1.call-update) | async-done | bytes 32784
  (24 shorter events, 4.1 us)
Async XLA Ops:
  9.2 22.3 %all-to-all-start = ((bf16[16,128,2,128]{3,2,1,0:T(2,128)(2,1)}), bf16[16,128,2,128]{3,2,1,0:T(2,128)(2,1)S(1)}, u32[]{:S(2)}, u32[]{:S(2)}) async-start(bf16[16,128,2,128]{3,2,1,0:T(2,128)(2,1)} %stack.14), calls=%async_computation | async-start | bytes 2097152 | tf_op jit(solution)/shard_map/all_to_all | solution.py:26
  15.0 221.8 %reduce-scatter.5.cloned.1.call-start = ((), (), s32[]{:S(2)}) async-start(), calls=%async_computation.3 | async-start | bytes 4456448 | tf_op jit(solution)/shard_map/reduce_scatter | solution.py:51
  137.5 10.0 %copy-start = (bf16[64,256,128]{1,2,0:T(8,128)(2,1)S(1)}, bf16[64,256,128]{1,2,0:T(8,128)(2,1)}, u32[]{:S(2)}) copy-start(bf16[64,256,128]{1,2,0:T(8,128)(2,1)} %fusion.18) | copy-start | bytes 12582916
  137.5 11.3 %copy-start.3 = (bf16[64,256,128]{1,2,0:T(8,128)(2,1)S(1)}, bf16[64,256,128]{1,2,0:T(8,128)(2,1)}, u32[]{:S(2)}) copy-start(bf16[64,256,128]{1,2,0:T(8,128)(2,1)} %get-tuple-element.8) | copy-start | bytes 12582916
  148.8 2.4 copy-start.2
  153.8 8.4 %copy-start.1 = (bf16[64,256,128]{2,1,0:T(8,128)(2,1)S(1)}, bf16[64,256,128]{2,1,0:T(8,128)(2,1)}, u32[]{:S(2)}) copy-start(bf16[64,256,128]{2,1,0:T(8,128)(2,1)} %fusion.16) | copy-start | bytes 12582916
  153.8 8.4 %copy-start.4 = (bf16[64,256,128]{2,1,0:T(8,128)(2,1)S(1)}, bf16[64,256,128]{2,1,0:T(8,128)(2,1)}, u32[]{:S(2)}) copy-start(bf16[64,256,128]{2,1,0:T(8,128)(2,1)} %get-tuple-element.5) | copy-start | bytes 12582916
  153.9 9.5 %copy-start.5 = (bf16[64,256,128]{2,1,0:T(8,128)(2,1)S(1)}, bf16[64,256,128]{2,1,0:T(8,128)(2,1)}, u32[]{:S(2)}) copy-start(bf16[64,256,128]{2,1,0:T(8,128)(2,1)} %get-tuple-element.6) | copy-start | bytes 12582916
  168.5 141.9 %reduce-scatter.7.cloned.1.call-start = ((), (), s32[]{:S(2)}) async-start(), calls=%async_computation.4 | async-start | bytes 294912
Sparse Core Ops, SparseCore 0:
  168.7 68.1 reduce-scatter.4
  240.8 69.6 reduce-scatter.6
